TPU v7x, 256 devices: a whole 4x4x8 slice. The times are simulated.
256 devices in a mesh: row: 8 (over z_hi, core), col: 32 (over x, z_lo, y).
Axes of the slice: x: 4, y: 4, z: 8 (z_hi: 4, z_lo: 2; z = z_hi * 2 + z_lo), core: 2. Of those that a mesh axis runs over, the one named last changes fastest.
Arguments:
- basis_out: float32 [16384, 16384], P('row', 'col'), may hold values from -0.046875 to 0.046875
- basis_in: float32 [16384, 16384], P('col', 'row'), may hold values from -0.046875 to 0.046875
- eig_damped: float32 [16384, 16384], P('col', 'row'), may hold values from 0.5 to 8
- query_left: bfloat16 [16384, 256], P(('row', 'col')), may hold values from -0.375 to 0.375
- query_right: bfloat16 [16384, 256], P('col'), may hold values from -6 to 6
- train_left: bfloat16 [16384, 512], P(('row', 'col')), may hold values from -0.046875 to 0.046875
- train_right: bfloat16 [16384, 512], P('col'), may hold values from -0.046875 to 0.046875
Outputs:
- response: float32 [16384, 512], P(('row', 'col'))
- scores: float32 [512], replicated
All inputs are finite; a program needn't handle non-finite values.
Results may differ from a plain program's by a relative error of at most 0.0003.
Values may be sent and summed in bfloat16 or wider, within the bound.
No kernel may reach another device: no remote copies, remote signals or barrier semaphores. Data moves between devices by JAX's collectives and lax.ppermute only.
A program may use at most 128 MiB of HBM per device.

v0:
```python
import jax
import jax.numpy as jnp
from jax import lax
from jax.sharding import Mesh
from jax.sharding import PartitionSpec as P

COL = ("col_0", "col_1", "col_2")
ROW = ("row_0", "row_1")
ROW_COL = ("row_0", "row_1", "col_0", "col_1", "col_2")


def joined_along(pieces, dim):
    dims = list(pieces.shape[1:])
    dims[dim] *= pieces.shape[0]
    return jnp.moveaxis(pieces, 0, dim).reshape(dims)


def from_everyone(array, axis):
    copies = jnp.broadcast_to(array, (lax.axis_size(axis), *array.shape))
    return lax.all_to_all(copies, axis, split_axis=0, concat_axis=0, tiled=True)


def gathered_copies(array, axis, dim):
    return joined_along(from_everyone(array, axis), dim)


def over_copies(array, axis):
    everything = from_everyone(array, axis)
    return jnp.sum(everything, axis=0)


def sum_in_order(pieces, axes, turns):
    dims = [lax.axis_size(a) for a in axes]
    pieces = pieces.reshape(*dims, *pieces.shape[1:])
    pieces = pieces.transpose(*turns, *range(len(axes), pieces.ndim))
    pieces = pieces.reshape(-1, *pieces.shape[len(axes) :])
    for k in turns:
        pieces = lax.psum_scatter(pieces, axes[k], scatter_dimension=0, tiled=True)
    return pieces[0]


def in_blocks(array, dim, devices):
    dims = array.shape
    pieces = array.reshape(*dims[:dim], devices, dims[dim] // devices, *dims[dim + 1 :])
    return jnp.moveaxis(pieces, dim, 0)


def summed_rows(array, axes, turns, dim):
    devices = lax.axis_size(axes)
    return sum_in_order(in_blocks(array, dim, devices), axes, turns)


def sent_and_summed(array, axis, dim):
    pieces = in_blocks(array, dim, lax.axis_size(axis))
    arrived = lax.all_to_all(pieces, axis, split_axis=0, concat_axis=0, tiled=True)
    return arrived.sum(axis=0)


def one_axis_at_a_time(array, axes):
    for axis in axes:
        array = lax.psum(array, axis)
    return array


def dot_first(left, right):
    return lax.dot_general(
        left,
        right,
        (((0,), (0,)), ((), ())),
        precision=lax.Precision.HIGHEST,
        preferred_element_type=jnp.float32,
    )


def dot_last(left, right):
    return lax.dot_general(
        left,
        right,
        (((1,), (1,)), ((), ())),
        precision=lax.Precision.HIGHEST,
        preferred_element_type=jnp.float32,
    )


def dot_plain(left, right):
    return jnp.dot(left, right, precision=lax.Precision.HIGHEST, preferred_element_type=jnp.float32)


def body(basis_out, basis_in, eig_damped, query_left, query_right, train_left, train_right):
    rank_width = query_right.shape[1]
    basis_rows = basis_out
    rot_left = dot_first(basis_rows, gathered_copies(query_left, COL, 0).astype(jnp.float32))
    rot_left = over_copies(rot_left, ROW)
    joined = jnp.concatenate([query_right, train_right], axis=1).astype(jnp.float32)
    share = summed_rows(dot_first(basis_in, joined), COL, (0, 2, 1), 0)
    piece = lax.all_gather(share, COL, axis=0, tiled=True)
    precond = dot_last(rot_left, piece[:, :rank_width]) / eig_damped
    contrib = dot_plain(precond, piece[:, rank_width:])
    applied = lax.psum(contrib, ROW)
    basis_rows = basis_out
    response = sent_and_summed(dot_plain(basis_rows, applied), COL, 0)
    partial_scores = jnp.sum(train_left.astype(jnp.float32) * response, axis=0)
    scores = one_axis_at_a_time(partial_scores, ROW_COL)
    return (response, scores)


def solution(mesh):
    finer = Mesh(mesh.devices.reshape(4, 2, 4, 2, 4), ("row_0", "row_1", "col_0", "col_1", "col_2"))
    placed = (
        P(ROW, COL),
        P(COL, ROW),
        P(COL, ROW),
        P(ROW_COL, None),
        P(COL, None),
        P(ROW_COL, None),
        P(COL, None),
    )
    return jax.shard_map(
        body, mesh=finer, in_specs=placed, out_specs=(P(ROW_COL, None), P()), check_vma=False
    )
```

profile of v0, /device:TPU:8, one launch (start us, length us, event | category | flops | bytes accessed | tf_op | source)
XLA Modules:
  0.0 579.2 jit_solution(16628478993421398997)
XLA Ops:
  7.2 0.0 reduce-scatter.4.cloned.1.call-start
  7.2 9.0 %convolution_bitcast_fusion = f32[2048,768]{0,1:T(8,128)} fusion(f32[512,2048]{1,0:T(8,128)} %param.8, bf16[512,512]{1,0:T(8,128)(2,1)} %param.13, bf16[512,256]{1,0:T(8,128)(2,1)} %param.11), kind=kOutput, calls=%fused_computation.3 | convolution fusion | flops 9665249280 | bytes 11272192 | tf_op jit(solution)/shard_map/dot_general | solution.py:66
  16.2 6.6 %copy.12 = f32[2048,768]{1,0:T(8,128)} copy(f32[2048,768]{0,1:T(8,128)} %convolution_bitcast_fusion) | data formatting | bytes 12582912 | tf_op jit(solution)/shard_map/dot_general | solution.py:66
  22.8 6.1 %copy.13 = f32[4,4,2,64,768]{4,3,2,1,0:T(8,128)} copy(f32[4,4,2,64,768]{4,3,1,2,0:T(8,128)} %bitcast.18) | data formatting | bytes 12582912 | tf_op jit(solution)/shard_map/transpose | solution.py:35
  28.9 0.0 reduce-scatter.4.cloned.1.call-update
  28.9 0.0 reduce-scatter.6.cloned.1.call-start
  29.0 69.5 %reduce-scatter.4.cloned.1.call-done = f32[8,64,768]{2,1,0:T(8,128)} async-done(((f32[32,64,768]{2,1,0:T(8,128)}), f32[8,64,768]{2,1,0:T(8,128)}) %reduce-scatter.4.cloned.1.call-update) | async-done | bytes 1572880 | tf_op jit(solution)/shard_map/reduce_scatter | solution.py:38
  98.5 0.0 reduce-scatter.6.cloned.1.call-update
  98.5 0.0 reduce-scatter.8.cloned.1.call-start
  98.6 29.4 %reduce-scatter.6.cloned.1.call-done = f32[2,64,768]{2,1,0:T(8,128)} async-done(((f32[8,64,768]{2,1,0:T(8,128)}), f32[2,64,768]{2,1,0:T(8,128)}) %reduce-scatter.6.cloned.1.call-update) | async-done | bytes 393232 | tf_op jit(solution)/shard_map/reduce_scatter | solution.py:38
  127.9 0.0 all-gather.3.cloned.1.call-start
  128.0 21.8 %reduce-scatter.8.cloned.1.call-done = f32[1,64,768]{2,1,0:T(8,128)} async-done(((f32[2,64,768]{2,1,0:T(8,128)}), f32[1,64,768]{2,1,0:T(8,128)}) %reduce-scatter.8.cloned.1.call-update) | async-done | bytes 196624 | tf_op jit(solution)/shard_map/reduce_scatter | solution.py:38
  149.8 0.0 all-reduce.2.cloned.1.call-start
  149.8 0.1 broadcast_in_dim.6
  150.0 25.1 %all_to_all.15 = bf16[32,64,256]{2,1,0:T(8,128)(2,1)S(1)} all-to-all(bf16[32,64,256]{2,1,0:T(8,128)(2,1)S(1)} %broadcast_in_dim.6), channel_id=1, replica_groups=mesh['row_0'=4,'row_1'=2,'col_0'=4,'col_1'=2,'col_2'=4] {'col_0','col_1'..., dimensions={0} | all-to-all | bytes 2097152 | tf_op jit(solution)/shard_map/all_to_all | solution.py:20
  175.1 5.7 fusion.9
  180.8 0.4 broadcast_in_dim.7
  181.2 103.8 %all_to_all.16 = f32[8,512,256]{2,1,0:T(8,128)} all-to-all(f32[8,512,256]{2,1,0:T(8,128)S(1)} %broadcast_in_dim.7), channel_id=1, replica_groups=mesh['row_0'=4,'row_1'=2,'col_0'=4,'col_1'=2,'col_2'=4] {'row_0','row_1'}, dimensions={0} | all-to-all | bytes 8388608 | tf_op jit(solution)/shard_map/all_to_all | solution.py:20
  284.9 2.5 reduce_sum.27
  287.5 71.0 %all-gather.3.cloned.1.call-done = f32[1,2048,768]{2,1,0:T(8,128)} async-done(((f32[1,64,768]{2,1,0:T(8,128)}), f32[1,2048,768]{2,1,0:T(8,128)}) %all-gather.3.cloned.1.call-update) | async-done | bytes 6291472 | tf_op jit(solution)/shard_map/all_gather | solution.py:96
  358.4 5.6 fusion.3
  364.1 10.3 %fusion = f32[512,512]{1,0:T(8,128)} fusion(f32[2048,768]{1,0:T(8,128)S(1)} %bitcast.22, f32[512,2048]{1,0:T(8,128)S(1)} %fusion.3, f32[512,2048]{1,0:T(8,128)} %param.9), kind=kOutput, calls=%fused_computation | convolution fusion | flops 6443499520 | bytes 13631488 | tf_op jit(solution)/shard_map/dot_general | solution.py:86
  374.4 78.1 %all-reduce.2.cloned.1.call-done = f32[512,512]{1,0:T(8,128)} async-done(((f32[512,512]{1,0:T(8,128)}), f32[512,512]{1,0:T(8,128)}) %all-reduce.2.cloned.1.call-update) | async-done | bytes 1048592 | tf_op jit(solution)/shard_map/psum | solution.py:99
  452.6 16.6 %convolution_bitcast_fusion.1 = f32[2048,512]{0,1:T(8,128)} fusion(f32[512,512]{1,0:T(8,128)} %all-reduce.2.cloned.1.call-done, f32[2048,512]{1,0:T(8,128)} %param.7), kind=kOutput, calls=%fused_computation.4 | convolution fusion | flops 6442450944 | bytes 9437184 | tf_op jit(solution)/shard_map/dot_general | solution.py:86
  469.2 5.3 copy.14
  474.6 56.6 %all_to_all.17 = f32[32,64,512]{2,1,0:T(8,128)} all-to-all(f32[32,64,512]{2,1,0:T(8,128)} %bitcast.19), channel_id=1, replica_groups=mesh['row_0'=4,'row_1'=2,'col_0'=4,'col_1'=2,'col_2'=4] {'col_0','col_1'..., dimensions={0} | all-to-all | bytes 8388608 | tf_op jit(solution)/shard_map/all_to_all | solution.py:55
  531.2 2.6 reduce_sum.28
  533.8 10.9 %psum.43 = f32[512]{0:T(512)S(1)} all-reduce(f32[512]{0:T(512)S(1)} %multiply_reduce_fusion), channel_id=1, replica_groups=mesh['row_0'=4,'row_1'=2,'col_0'=4,'col_1'=2,'col_2'=4] {'row_0'}, use_global_device_ids=true, to_apply=%region_7.0 | all-reduce | flops 512 | bytes 4096 | tf_op jit(solution)/shard_map/psum | solution.py:61
  544.7 2.5 psum.44
  547.2 8.7 %psum.45 = f32[512]{0:T(512)S(1)} all-reduce(f32[512]{0:T(512)S(1)} %psum.44), channel_id=1, replica_groups=mesh['row_0'=4,'row_1'=2,'col_0'=4,'col_1'=2,'col_2'=4] {'col_0'}, use_global_device_ids=true, to_apply=%region_9.0 | all-reduce | flops 512 | bytes 4096 | tf_op jit(solution)/shard_map/psum | solution.py:61
  555.9 4.9 psum.46
  560.8 11.8 %psum.47 = f32[512]{0:T(512)} all-reduce(f32[512]{0:T(512)S(1)} %psum.46), channel_id=1, replica_groups=mesh['row_0'=4,'row_1'=2,'col_0'=4,'col_1'=2,'col_2'=4] {'col_2'}, use_global_device_ids=true, to_apply=%region_11.0 | all-reduce | flops 512 | bytes 4096 | tf_op jit(solution)/shard_map/psum | solution.py:61
  (12 shorter events, 0.1 us)
Async XLA Ops:
  7.2 91.3 %reduce-scatter.4.cloned.1.call-start = ((), (), s32[]{:S(2)}) async-start(), calls=%async_computation.6 | async-start | bytes 7864320 | tf_op jit(solution)/shard_map/reduce_scatter | solution.py:38
  28.9 120.9 %copy-start.3 = (bf16[64,256]{1,0:T(8,128)(2,1)S(1)}, bf16[64,256]{1,0:T(8,128)(2,1)}, u32[]{:S(2)}) copy-start(bf16[64,256]{1,0:T(8,128)(2,1)} %param.10) | copy-start | bytes 98308
  28.9 99.0 %reduce-scatter.6.cloned.1.call-start = ((), (), s32[]{:S(2)}) async-start(), calls=%async_computation.7 | async-start | bytes 1966080 | tf_op jit(solution)/shard_map/reduce_scatter | solution.py:38
  98.5 51.3 %reduce-scatter.8.cloned.1.call-start = ((), (), s32[]{:S(2)}) async-start(), calls=%async_computation.8 | async-start | bytes 589824 | tf_op jit(solution)/shard_map/reduce_scatter | solution.py:38
  127.9 230.5 %all-gather.3.cloned.1.call-start = ((), (), s32[]{:S(2)}) async-start(), calls=%async_computation.10 | async-start | bytes 6488064 | tf_op jit(solution)/shard_map/all_gather | solution.py:96
  149.8 302.8 %all-reduce.2.cloned.1.call-start = ((), (), s32[]{:S(2)}) async-start(), calls=%async_computation.9 | async-start | bytes 2097152 | tf_op jit(solution)/shard_map/psum | solution.py:99
  358.4 5.6 copy-start
  531.2 2.6 copy-start.2
  533.7 38.9 %copy-start.1 = (f32[64,512]{1,0:T(8,128)}, f32[64,512]{1,0:T(8,128)S(1)}, u32[]{:S(2)}) copy-start(f32[64,512]{1,0:T(8,128)S(1)} %reduce_sum.28) | copy-start | bytes 393220
Sparse Core Ops, SparseCore 0:
  29.1 69.3 reduce-scatter.3
  101.0 26.8 reduce-scatter.5
  130.4 19.3 reduce-scatter.7
  151.4 206.9 all-gather.2
  374.6 77.9 all-reduce.1
where the time goes:
time: 580 us; the launch traced here: 579 us
  waiting for transfers between devices  270 us (47%)
  blocking collectives  224 us (39%)
  matrix products  47.3 us (8%)
  local copies, waits for them, and re-layouts  18.6 us (3%)
  between operations  13.9 us (2%)
    all_to_all x2, blocking collectives, from_everyone(): return lax.all_to_all(copies, axis, split_axis=0, concat_axis=0, tiled=True)  129 us
    reduce_scatter x3, waiting for transfers between devices, sum_in_order(): pieces = lax.psum_scatter(pieces, axes[k], scatter_dimension=0, tiled=True)  121 us
    psum x1, waiting for transfers between devices, body(): applied = lax.psum(contrib, ROW)  78.1 us
    all_gather x1, waiting for transfers between devices, body(): piece = lax.all_gather(share, COL, axis=0, tiled=True)  71 us
    all_to_all x1, blocking collectives, sent_and_summed(): lax.all_to_all(pieces, axis, split_axis=0, concat_axis=0, tiled=True)  56.6 us
    psum x5, blocking collectives, one_axis_at_a_time(): array = lax.psum(array, axis)  38.9 us
    dot_general x2, matrix products, dot_plain(): jnp.dot(left, right, precision=lax.Precision.HIGHEST, preferred_element_t...  27 us
    dot_general x2, matrix products, dot_first(): lax.dot_general(left, right, (((0,), (0,)), ((), ())), precision=lax.Prec...  14.7 us
  transfers between devices with their start and end apart: 5, of which 5 were waited for; matrix products, arithmetic and copies ran while one was open for 2% of the time, Pallas kernels for 0%

commit v1 on v0

--- a/solution.py
+++ b/solution.py
@@ -93,7 +93,8 @@
     rot_left = over_copies(rot_left, ROW)
     joined = jnp.concatenate([query_right, train_right], axis=1).astype(jnp.float32)
     share = summed_rows(dot_first(basis_in, joined), COL, (0, 2, 1), 0)
-    piece = lax.all_gather(share, COL, axis=0, tiled=True)
+    stack = jnp.stack([share] * lax.axis_size(COL))
+    piece = jnp.concatenate(lax.all_to_all(stack, COL, 0, 0), axis=0)
     precond = dot_last(rot_left, piece[:, :rank_width]) / eig_damped
     contrib = dot_plain(precond, piece[:, rank_width:])
     applied = lax.psum(contrib, ROW)

time: 580 us -> 502 us (0.87)
  blocking collectives: 224 us -> 123 us
  starting transfers between devices: 0.19 us -> 17 us
  local copies, waits for them, and re-layouts: 18.6 us -> 25.5 us
    all_to_all x0 -> x2, waiting for transfers between devices: none -> 126 us  [the longest x1 90.6 us: body(): piece = jnp.concatenate(lax.all_to_all(stack, COL, 0, 0), axis=0)]
    all_to_all x2 -> x1, blocking collectives: 129 us -> 27.2 us  [from_everyone(): return lax.all_to_all(copies, axis, split_axis=0, concat_axis=0, tiled=True)]
    all_gather x1 -> x0, waiting for transfers between devices: 71 us -> none  [body(): piece = lax.all_gather(share, COL, axis=0, tiled=True)]
    reduce_scatter x3, waiting for transfers between devices: 121 us -> 63.3 us  [sum_in_order(): pieces = lax.psum_scatter(pieces, axes[k], scatter_dimension=0, tiled=True)]
    all_to_all x0 -> x2, starting transfers between devices: none -> 16.6 us  [the longest x1 8.8 us: body(): piece = jnp.concatenate(lax.all_to_all(stack, COL, 0, 0), axis=0)]
  transfers between devices with their start and end apart: 5 -> 6, of which waited for: 5 -> 6; matrix products, arithmetic and copies ran while one was open for 2% -> 2% of each run, Pallas kernels for 0% -> 0%
where the time goes in v1:
time: 502 us
  waiting for transfers between devices  271 us (54%)
  blocking collectives  123 us (25%)
  matrix products  46.7 us (9%)
  local copies, waits for them, and re-layouts  25.5 us (5%)
  starting transfers between devices  17 us (3%)
  between operations  13.8 us (3%)
  other arithmetic  5.12 us (1%)
    all_to_all x1, waiting for transfers between devices, body(): piece = jnp.concatenate(lax.all_to_all(stack, COL, 0, 0), axis=0)  90.6 us
    psum x1, waiting for transfers between devices, body(): applied = lax.psum(contrib, ROW)  81.9 us
    reduce_scatter x3, waiting for transfers between devices, sum_in_order(): pieces = lax.psum_scatter(pieces, axes[k], scatter_dimension=0, tiled=True)  63.3 us
    all_to_all x1, blocking collectives, sent_and_summed(): lax.all_to_all(pieces, axis, split_axis=0, concat_axis=0, tiled=True)  56.6 us
    psum x5, blocking collectives, one_axis_at_a_time(): array = lax.psum(array, axis)  38.9 us
    all_to_all x1, waiting for transfers between devices, from_everyone(): return lax.all_to_all(copies, axis, split_axis=0, concat_axis=0, tiled=True)  35 us
    all_to_all x1, blocking collectives, from_everyone(): return lax.all_to_all(copies, axis, split_axis=0, concat_axis=0, tiled=True)  27.2 us
    dot_general x2, matrix products, dot_plain(): jnp.dot(left, right, precision=lax.Precision.HIGHEST, preferred_element_t...  26.4 us
  transfers between devices with their start and end apart: 6, of which 6 were waited for; matrix products, arithmetic and copies ran while one was open for 2% of the time, Pallas kernels for 0%

profile of v1, /device:TPU:8, one launch (start us, length us, event | category | flops | bytes accessed | tf_op | source)
XLA Modules:
  0.0 501.6 jit_solution(13159863466746664863)
XLA Ops:
  7.2 0.0 reduce-scatter.4.cloned.1.call-start
  7.2 8.9 %convolution_bitcast_fusion = f32[2048,768]{0,1:T(8,128)} fusion(f32[512,2048]{1,0:T(8,128)} %param.8, bf16[512,512]{1,0:T(8,128)(2,1)} %param.13, bf16[512,256]{1,0:T(8,128)(2,1)} %param.11), kind=kOutput, calls=%fused_computation.3 | convolution fusion | flops 9665249280 | bytes 11272192 | tf_op jit(solution)/shard_map/dot_general | solution.py:66
  16.1 6.5 %copy.12 = f32[2048,768]{1,0:T(8,128)} copy(f32[2048,768]{0,1:T(8,128)} %convolution_bitcast_fusion) | data formatting | bytes 12582912 | tf_op jit(solution)/shard_map/dot_general | solution.py:66
  22.6 6.1 %copy.13 = f32[4,4,2,64,768]{4,3,2,1,0:T(8,128)} copy(f32[4,4,2,64,768]{4,3,1,2,0:T(8,128)} %bitcast.19) | data formatting | bytes 12582912 | tf_op jit(solution)/shard_map/transpose | solution.py:35
  28.7 0.7 copy-done.2
  29.5 0.1 broadcast_in_dim.6
  29.6 27.2 %all_to_all.20 = bf16[32,64,256]{2,1,0:T(8,128)(2,1)S(1)} all-to-all(bf16[32,64,256]{2,1,0:T(8,128)(2,1)S(1)} %broadcast_in_dim.6), channel_id=1, replica_groups=mesh['row_0'=4,'row_1'=2,'col_0'=4,'col_1'=2,'col_2'=4] {'col_0','col_1'..., dimensions={0} | all-to-all | bytes 2097152 | tf_op jit(solution)/shard_map/all_to_all | solution.py:20
  56.8 5.8 %fusion.9 = f32[512,256]{1,0:T(8,128)S(1)} fusion(f32[2048,512]{1,0:T(8,128)} %param.7, bf16[2048,256]{1,0:T(8,128)(2,1)S(1)} %bitcast.21), kind=kOutput, calls=%fused_computation.12 | convolution fusion | flops 3221225472 | bytes 5767168 | tf_op jit(solution)/shard_map/dot_general | solution.py:66
  62.7 2.4 broadcast_in_dim.7
  65.0 7.8 %all-to-all-start.1 = ((f32[8,512,256]{2,1,0:T(8,128)}), f32[8,512,256]{2,1,0:T(8,128)}, u32[]{:S(2)}, u32[]{:S(2)}) async-start(f32[8,512,256]{2,1,0:T(8,128)} %broadcast_in_dim.7), calls=%async_computation.1 | async-start | bytes 8388608 | tf_op jit(solution)/shard_map/all_to_all | solution.py:20
  72.9 31.8 %reduce-scatter.4.cloned.1.call-done = f32[8,64,768]{2,1,0:T(8,128)} async-done(((f32[32,64,768]{2,1,0:T(8,128)}), f32[8,64,768]{2,1,0:T(8,128)}) %reduce-scatter.4.cloned.1.call-update) | async-done | bytes 1572880 | tf_op jit(solution)/shard_map/reduce_scatter | solution.py:38
  104.8 0.0 reduce-scatter.8.cloned.1.call-start
  104.8 29.9 %reduce-scatter.6.cloned.1.call-done = f32[2,64,768]{2,1,0:T(8,128)} async-done(((f32[8,64,768]{2,1,0:T(8,128)}), f32[2,64,768]{2,1,0:T(8,128)}) %reduce-scatter.6.cloned.1.call-update) | async-done | bytes 393232 | tf_op jit(solution)/shard_map/reduce_scatter | solution.py:38
  134.7 35.0 %all-to-all-done.1 = f32[8,512,256]{2,1,0:T(8,128)} async-done(((f32[8,512,256]{2,1,0:T(8,128)}), f32[8,512,256]{2,1,0:T(8,128)}, u32[]{:S(2)}, u32[]{:S(2)}) %all-to-all-start.1) | async-done | bytes 4194336 | tf_op jit(solution)/shard_map/all_to_all | solution.py:20
  169.7 1.6 reduce-scatter.8.cloned.1.call-done
  171.3 4.3 stack.3
  175.6 8.8 %all-to-all-start.2 = ((f32[32,64,768]{2,1,0:T(8,128)}), f32[32,64,768]{2,1,0:T(8,128)}, u32[]{:S(2)}, u32[]{:S(2)}) async-start(f32[32,64,768]{2,1,0:T(8,128)} %stack.3), calls=%async_computation.5 | async-start | bytes 12582912 | tf_op jit(solution)/shard_map/all_to_all | solution.py:97
  184.4 0.2 all-reduce.2.cloned.1.call-start
  184.6 2.5 reduce_sum.27
  187.1 90.6 %all-to-all-done.2 = f32[32,64,768]{2,1,0:T(8,128)} async-done(((f32[32,64,768]{2,1,0:T(8,128)}), f32[32,64,768]{2,1,0:T(8,128)}, u32[]{:S(2)}, u32[]{:S(2)}) %all-to-all-start.2) | async-done | bytes 6291488 | tf_op jit(solution)/shard_map/all_to_all | solution.py:97
  277.7 5.6 %fusion.3 = f32[512,2048]{1,0:T(8,128)S(1)} fusion(f32[512,256]{1,0:T(8,128)S(1)} %reduce_sum.27, f32[2048,768]{1,0:T(8,128)} %bitcast.6), kind=kOutput, calls=%fused_computation.5 | convolution fusion | flops 3221225472 | bytes 6815744 | tf_op jit(solution)/shard_map/dot_general | solution.py:76
  283.4 9.7 %fusion = f32[512,512]{1,0:T(8,128)} fusion(f32[2048,768]{1,0:T(8,128)} %bitcast.6, f32[512,2048]{1,0:T(8,128)S(1)} %fusion.3, f32[512,2048]{1,0:T(8,128)S(1)} %copy-done.3), kind=kOutput, calls=%fused_computation | convolution fusion | flops 6443499520 | bytes 13631488 | tf_op jit(solution)/shard_map/dot_general | solution.py:86
  293.1 81.9 %all-reduce.2.cloned.1.call-done = f32[512,512]{1,0:T(8,128)} async-done(((f32[512,512]{1,0:T(8,128)}), f32[512,512]{1,0:T(8,128)}) %all-reduce.2.cloned.1.call-update) | async-done | bytes 1048592 | tf_op jit(solution)/shard_map/psum | solution.py:100
  375.0 16.6 %convolution_bitcast_fusion.1 = f32[2048,512]{0,1:T(8,128)} fusion(f32[512,512]{1,0:T(8,128)} %all-reduce.2.cloned.1.call-done, f32[2048,512]{1,0:T(8,128)} %param.7), kind=kOutput, calls=%fused_computation.4 | convolution fusion | flops 6442450944 | bytes 9437184 | tf_op jit(solution)/shard_map/dot_general | solution.py:86
  391.6 5.3 %copy.14 = f32[2048,512]{1,0:T(8,128)} copy(f32[2048,512]{0,1:T(8,128)} %convolution_bitcast_fusion.1) | data formatting | bytes 8388608 | tf_op jit(solution)/shard_map/dot_general | solution.py:86
  397.0 56.6 %all_to_all.21 = f32[32,64,512]{2,1,0:T(8,128)} all-to-all(f32[32,64,512]{2,1,0:T(8,128)} %bitcast.20), channel_id=1, replica_groups=mesh['row_0'=4,'row_1'=2,'col_0'=4,'col_1'=2,'col_2'=4] {'col_0','col_1'..., dimensions={0} | all-to-all | bytes 8388608 | tf_op jit(solution)/shard_map/all_to_all | solution.py:55
  453.6 2.6 reduce_sum.28
  456.2 10.9 %psum.43 = f32[512]{0:T(512)S(1)} all-reduce(f32[512]{0:T(512)S(1)} %multiply_reduce_fusion), channel_id=1, replica_groups=mesh['row_0'=4,'row_1'=2,'col_0'=4,'col_1'=2,'col_2'=4] {'row_0'}, use_global_device_ids=true, to_apply=%region_7.0 | all-reduce | flops 512 | bytes 4096 | tf_op jit(solution)/shard_map/psum | solution.py:61
  467.1 2.5 psum.44
  469.6 8.7 %psum.45 = f32[512]{0:T(512)S(1)} all-reduce(f32[512]{0:T(512)S(1)} %psum.44), channel_id=1, replica_groups=mesh['row_0'=4,'row_1'=2,'col_0'=4,'col_1'=2,'col_2'=4] {'col_0'}, use_global_device_ids=true, to_apply=%region_9.0 | all-reduce | flops 512 | bytes 4096 | tf_op jit(solution)/shard_map/psum | solution.py:61
  478.3 4.9 psum.46
  483.2 11.8 %psum.47 = f32[512]{0:T(512)} all-reduce(f32[512]{0:T(512)S(1)} %psum.46), channel_id=1, replica_groups=mesh['row_0'=4,'row_1'=2,'col_0'=4,'col_1'=2,'col_2'=4] {'col_2'}, use_global_device_ids=true, to_apply=%region_11.0 | all-reduce | flops 512 | bytes 4096 | tf_op jit(solution)/shard_map/psum | solution.py:61
  (13 shorter events, 0.2 us)
Async XLA Ops:
  7.2 97.6 %reduce-scatter.4.cloned.1.call-start = ((), (), s32[]{:S(2)}) async-start(), calls=%async_computation.7 | async-start | bytes 7864320 | tf_op jit(solution)/shard_map/reduce_scatter | solution.py:38
  28.7 0.8 copy-start.2
  65.0 104.7 %all-to-all-start.1 = ((f32[8,512,256]{2,1,0:T(8,128)}), f32[8,512,256]{2,1,0:T(8,128)}, u32[]{:S(2)}, u32[]{:S(2)}) async-start(f32[8,512,256]{2,1,0:T(8,128)} %broadcast_in_dim.7), calls=%async_computation.1 | async-start | bytes 8388608 | tf_op jit(solution)/shard_map/all_to_all | solution.py:20
  72.9 61.8 %reduce-scatter.6.cloned.1.call-start = ((), (), s32[]{:S(2)}) async-start(), calls=%async_computation.8 | async-start | bytes 1966080 | tf_op jit(solution)/shard_map/reduce_scatter | solution.py:38
  104.8 66.5 %reduce-scatter.8.cloned.1.call-start = ((), (), s32[]{:S(2)}) async-start(), calls=%async_computation.9 | async-start | bytes 589824 | tf_op jit(solution)/shard_map/reduce_scatter | solution.py:38
  175.6 102.2 %all-to-all-start.2 = ((f32[32,64,768]{2,1,0:T(8,128)}), f32[32,64,768]{2,1,0:T(8,128)}, u32[]{:S(2)}, u32[]{:S(2)}) async-start(f32[32,64,768]{2,1,0:T(8,128)} %stack.3), calls=%async_computation.5 | async-start | bytes 12582912 | tf_op jit(solution)/shard_map/all_to_all | solution.py:97
  184.4 190.6 %all-reduce.2.cloned.1.call-start = ((), (), s32[]{:S(2)}) async-start(), calls=%async_computation.10 | async-start | bytes 2097152 | tf_op jit(solution)/shard_map/psum | solution.py:100
  277.7 5.6 %copy-start.3 = (f32[512,2048]{1,0:T(8,128)S(1)}, f32[512,2048]{1,0:T(8,128)}, u32[]{:S(2)}) copy-start(f32[512,2048]{1,0:T(8,128)} %param.9) | copy-start | bytes 12582916
  453.6 2.6 copy-start.1
  456.2 38.9 %copy-start = (f32[64,512]{1,0:T(8,128)}, f32[64,512]{1,0:T(8,128)S(1)}, u32[]{:S(2)}) copy-start(f32[64,512]{1,0:T(8,128)S(1)} %reduce_sum.28) | copy-start | bytes 393220
Sparse Core Ops, SparseCore 0:
  28.9 75.8 reduce-scatter.3
  107.3 27.3 reduce-scatter.5
  137.2 34.0 reduce-scatter.7
  293.2 81.6 all-reduce.1
